TPU v7x, 32 devices: a whole 2x2x4 slice. The times are simulated.
32 devices in a mesh: seq: 8 (over y, x, core), tp: 4 (over z).
Axes of the slice: x: 2, y: 2, z: 4, core: 2. Of those that a mesh axis runs over, the one named last changes fastest.
Arguments:
- features: bfloat16 [576, 5376], P('seq', 'tp'), may hold values from -6 to 6
- gate_logits: float32 [1, 3], replicated, may hold values from -3 to 3
- proj_weight: bfloat16 [5376, 8192], P('tp'), may hold values from -0.125 to 0.125
- positions: int32 [576], replicated, may hold values from 0 to 12287, as said below
- text: bfloat16 [12288, 8192], P(('seq', 'tp')), may hold values from -6 to 6
Outputs:
- mixed: bfloat16 [12288, 8192], P(('seq', 'tp'))
Inputs may be any that keep to these rules, and one draw needn't show every extreme that they name: All positions are distinct. Of the 72 image tokens of one index of seq (rows of an aligned block), at most 9 fall into one aligned block of 1536 positions, and exactly 9 do for some pair of blocks. At most 18 image tokens in all fall into one aligned block of 384 positions, and exactly 18 do in the first such block of every aligned block of 1536 positions.
All inputs are finite; a program needn't handle non-finite values.
Results may differ from a plain program's by a relative error of at most 0.005.
Values may be sent and summed in bfloat16 or wider, within the bound.
A program may use at most 64 MiB of HBM per device.

v0:
```python
import jax
import jax.numpy as jnp
from jax import lax
from jax.sharding import PartitionSpec as P

CLIP_C = 1024
CNX_C = 3072
SIDE = 24
TOK_DEV = 1536


def gate_features(features, gate_logits):
    rows, width = features.shape
    first_row = lax.axis_index("seq") * rows
    image_ids = (first_row + jnp.arange(rows, dtype=jnp.int32)) // (SIDE * SIDE)
    pick = image_ids[:, None] == jnp.arange(gate_logits.shape[0], dtype=jnp.int32)[None, :]
    row_logits = jnp.sum(jnp.where(pick[:, :, None], gate_logits[None, :, :], 0.0), axis=1)
    row_gates = jax.nn.sigmoid(row_logits)
    channel = lax.axis_index("tp") * width + jnp.arange(width, dtype=jnp.int32)
    encoder = (channel >= CLIP_C).astype(jnp.int32) + (channel >= CLIP_C + CNX_C).astype(jnp.int32)
    gates = jnp.where(
        encoder[None, :] == 0,
        row_gates[:, 0:1],
        jnp.where(encoder[None, :] == 1, row_gates[:, 1:2], row_gates[:, 2:3]),
    )
    return (features.astype(jnp.float32) * gates).astype(jnp.bfloat16)


def shards(features, gate_logits, proj_weight, positions, text):
    seq_count = lax.axis_size("seq")
    tp_count = lax.axis_size("tp")
    per_device = features.shape[0]
    capacity = -(-per_device // seq_count)
    slot_total = seq_count * capacity
    sub_capacity = -(-slot_total // tp_count)
    own_index = lax.axis_index("seq")
    target_grid = (positions // TOK_DEV).reshape(seq_count, per_device)
    offset_grid = (positions % TOK_DEV).reshape(seq_count, per_device)
    row_order = jnp.arange(per_device, dtype=jnp.int32)
    earlier = (target_grid[:, :, None] == target_grid[:, None, :]) & (
        row_order[None, None, :] < row_order[None, :, None]
    )
    slot_grid = jnp.sum(earlier.astype(jnp.int32), axis=2)
    own_target = lax.dynamic_index_in_dim(target_grid, own_index, 0, keepdims=False)
    own_slot = lax.dynamic_index_in_dim(slot_grid, own_index, 0, keepdims=False)
    choose = (
        (own_target * capacity + own_slot)[None, :]
        == jnp.arange(slot_total, dtype=jnp.int32)[:, None]
    ).astype(jnp.bfloat16)
    match = (target_grid[:, None, :] == own_index) & (
        slot_grid[:, None, :] == jnp.arange(capacity, dtype=jnp.int32)[None, :, None]
    )
    arrived_offset = (
        jnp.sum(jnp.where(match, offset_grid[:, None, :] + 1, 0), axis=2) - 1
    ).reshape(slot_total)
    rows_here = text.shape[0]
    valid = arrived_offset >= 0
    sub_block = jnp.where(valid, arrived_offset // rows_here, -1)
    slot_ids = jnp.arange(slot_total, dtype=jnp.int32)
    same_before = (sub_block[:, None] == sub_block[None, :]) & (
        slot_ids[None, :] < slot_ids[:, None]
    )
    sub_rank = jnp.sum(same_before.astype(jnp.int32), axis=1)
    slot_row = jnp.where(valid, sub_block * sub_capacity + sub_rank, -1)
    gated = gate_features(features, gate_logits)
    outgoing = jnp.dot(choose, gated, preferred_element_type=jnp.float32).astype(jnp.bfloat16)
    arrived = lax.all_to_all(outgoing, "seq", split_axis=0, concat_axis=0, tiled=True)
    wanted = jnp.arange(sub_capacity * lax.axis_size("tp"), dtype=jnp.int32)
    picking = (slot_row[None, :] == wanted[:, None]).astype(jnp.bfloat16)
    picked = jnp.dot(picking, arrived, preferred_element_type=jnp.float32).astype(jnp.bfloat16)
    projected = jnp.dot(picked, proj_weight, preferred_element_type=jnp.float32).astype(
        jnp.bfloat16
    )
    summed = lax.psum_scatter(
        lax.optimization_barrier(projected).astype(jnp.float32).astype(jnp.bfloat16),
        "tp",
        scatter_dimension=0,
        tiled=True,
    )
    own_block = lax.axis_index("tp")
    local_row = arrived_offset - own_block * rows_here
    mine = sub_block == own_block
    rank_match = mine[None, :] & (
        sub_rank[None, :] == jnp.arange(sub_capacity, dtype=jnp.int32)[:, None]
    )
    row_of = jnp.sum(jnp.where(rank_match, local_row[None, :] + 1, 0), axis=1) - 1
    wanted_rows = jnp.arange(rows_here, dtype=jnp.int32)
    hits = row_of[None, :] == wanted_rows[:, None]
    placing = hits.astype(jnp.bfloat16)
    placed = jnp.dot(placing, summed, preferred_element_type=jnp.float32).astype(jnp.bfloat16)
    filled = jnp.any(hits, axis=1)
    return jnp.where(filled[:, None], placed, text)


def solution(mesh):
    return jax.shard_map(
        shards,
        mesh=mesh,
        in_specs=(P("seq", "tp"), P(), P("tp", None), P(), P(("seq", "tp"), None)),
        out_specs=P(("seq", "tp"), None),
        check_vma=False,
    )
```

profile of v0, /device:TPU:0, one launch (start us, length us, event | category | flops | bytes accessed | tf_op | source)
XLA Modules:
  0.0 75.8 jit_solution(260586676349018159)
XLA Ops:
  0.0 0.7 add_divide_fusion.1
  0.8 0.7 add_select_fusion.1
  1.5 0.1 broadcast_in_dim_reshape.2
  1.6 0.3 convert_reduce_fusion
  1.9 1.3 %convolution_convert_fusion.3 = bf16[72,1344]{1,0:T(8,128)(2,1)S(1)} fusion(bf16[72,1344]{1,0:T(8,128)(2,1)} %param.5, f32[72]{0:T(128)S(1)} %get-tuple-element.14, f32[72]{0:T(128)S(1)} %get-tuple-element.15, f32[72]{0:T(128)S(1)} %get-tuple-element.13, pred[1344]{0:T(1024)(128)(4,1)S(1)} %get-tuple-element.16, pred[1344]{0:T(1024)(128)(4,1)S(1)} %get-tuple-element.17, ...), kind=kOutput, calls=%fused_computation.4 | convolution fusion | flops 14520384 | bytes 390912 | tf_op jit(solution)/shard_map/dot_general | solution.py:66
  3.2 0.8 %all_to_all.8 = bf16[8,9,1344]{2,1,0:T(8,128)(2,1)} reshape(bf16[72,1344]{1,0:T(8,128)(2,1)S(1)} %convolution_convert_fusion.3) | data formatting | bytes 387072 | tf_op jit(solution)/shard_map/all_to_all | solution.py:67
  4.0 5.2 %all-to-all-start = ((bf16[8,9,1344]{2,1,0:T(8,128)(2,1)}), bf16[8,9,1344]{2,1,0:T(8,128)(2,1)S(1)}, u32[]{:S(2)}, u32[]{:S(2)}) async-start(bf16[8,9,1344]{2,1,0:T(8,128)(2,1)} %all_to_all.8), calls=%async_computation | async-start | bytes 720896 | tf_op jit(solution)/shard_map/all_to_all | solution.py:67
  9.2 0.1 add.134
  9.3 0.2 select_reduce_fusion
  9.6 0.1 copy.10
  9.7 0.1 and.73
  9.7 0.1 ge.53
  9.8 0.1 div.43
  9.9 0.2 convert_reduce_fusion.1
  10.1 0.1 add.136
  10.2 1.3 %dynamic-slice.4 = u32[1]{0:T(128)} dynamic-slice(u32[32]{0:T(128)} %constant.82, u32[]{:S(6)} %partition-id.4), dynamic_slice_sizes={1} | dynamic-slice | bytes 12
  12.2 0.1 select_reduce_fusion.1
  12.4 4.8 %all-to-all-done = bf16[8,9,1344]{2,1,0:T(8,128)(2,1)S(1)} async-done(((bf16[8,9,1344]{2,1,0:T(8,128)(2,1)}), bf16[8,9,1344]{2,1,0:T(8,128)(2,1)S(1)}, u32[]{:S(2)}, u32[]{:S(2)}) %all-to-all-start) | async-done | bytes 193568 | tf_op jit(solution)/shard_map/all_to_all | solution.py:67
  17.2 0.1 all_to_all.10
  17.3 9.5 %convolution_convert_fusion.1 = bf16[72,8192]{1,0:T(8,128)(2,1)S(1)} fusion(bf16[1344,8192]{1,0:T(8,128)(2,1)} %param.7, bf16[72,1344]{1,0:T(8,128)(2,1)S(1)} %all_to_all.10, s32[72]{0:T(128)S(1)} %add_select_fusion.3), kind=kOutput, calls=%fused_computation.2 | convolution fusion | flops 1600073216 | bytes 23393568 | tf_op jit(solution)/shard_map/dot_general | solution.py:71
  26.9 33.1 %fusion = bf16[24,8192]{1,0:T(8,128)(2,1)S(1)} fusion(bf16[72,8192]{1,0:T(8,128)(2,1)S(1)} %convolution_convert_fusion.1), kind=kCustom, calls=%all-reduce-scatter | all-reduce-scatter fusion | flops 786433 | bytes 1573376
  60.0 0.1 slice.12
  60.1 1.3 %collective-permute-start = (bf16[18,8192]{1,0:T(8,128)(2,1)S(1)}, bf16[18,8192]{1,0:T(8,128)(2,1)S(1)}, u32[]{:S(2)}, u32[]{:S(2)}) collective-permute-start(bf16[18,8192]{1,0:T(8,128)(2,1)S(1)} %slice.12), channel_id=1, source_target_pairs={{0,1},{1,2},{2,3},{4,5},{5,6},{6,7},{8,9},{9,10},{10,11},{12,13},{... | collective-permute-start | bytes 884744
  61.4 0.1 fusion.8
  61.5 6.0 %collective-permute-done = bf16[18,8192]{1,0:T(8,128)(2,1)S(1)} collective-permute-done((bf16[18,8192]{1,0:T(8,128)(2,1)S(1)}, bf16[18,8192]{1,0:T(8,128)(2,1)S(1)}, u32[]{:S(2)}, u32[]{:S(2)}) %collective-permute-start) | collective-permute-done | bytes 294944
  67.5 0.8 %concatenate = bf16[42,8192]{1,0:T(8,128)(2,1)S(1)} concatenate(bf16[18,8192]{1,0:T(8,128)(2,1)S(1)} %collective-permute-done, bf16[24,8192]{1,0:T(8,128)(2,1)S(1)} %fusion), dimensions={0} | concatenate | bytes 1376256
  68.4 7.4 %fusion.1 = bf16[384,8192]{1,0:T(8,128)(2,1)} fusion(bf16[384,8192]{1,0:T(8,128)(2,1)} %param.9, pred[384]{0:T(512)(128)(4,1)S(1)} %fusion.8, bf16[42,8192]{1,0:T(8,128)(2,1)S(1)} %concatenate, u32[]{:S(6)} %subtract, s32[18]{0:T(128)S(1)} %broadcast_add_fusion), kind=kOutput, calls=%fused_computation.1 | convolution fusion | flops 119544576 | bytes 12977156 | tf_op jit(solution)/shard_map/dot_general | solution.py:90
  (11 shorter events, 0.1 us)
Async XLA Ops:
  4.0 13.2 %all-to-all-start = ((bf16[8,9,1344]{2,1,0:T(8,128)(2,1)}), bf16[8,9,1344]{2,1,0:T(8,128)(2,1)S(1)}, u32[]{:S(2)}, u32[]{:S(2)}) async-start(bf16[8,9,1344]{2,1,0:T(8,128)(2,1)} %all_to_all.8), calls=%async_computation | async-start | bytes 720896 | tf_op jit(solution)/shard_map/all_to_all | solution.py:67
  60.1 7.4 %collective-permute-start = (bf16[18,8192]{1,0:T(8,128)(2,1)S(1)}, bf16[18,8192]{1,0:T(8,128)(2,1)S(1)}, u32[]{:S(2)}, u32[]{:S(2)}) collective-permute-start(bf16[18,8192]{1,0:T(8,128)(2,1)S(1)} %slice.12), channel_id=1, source_target_pairs={{0,1},{1,2},{2,3},{4,5},{5,6},{6,7},{8,9},{9,10},{10,11},{12,13},{... | collective-permute-start | bytes 884744
where the time goes:
time: 77.3 us; the launch traced here: 75.8 us
  blocking collectives  33.1 us (43%)
  matrix products  18.2 us (24%)
  waiting for transfers between devices  10.8 us (14%)
  starting transfers between devices  6.51 us (8%)
  local copies, waits for them, and re-layouts  3.75 us (5%)
  other arithmetic  2.51 us (3%)
  between operations  0.83 us (1%)
    unnamed x1, blocking collectives  33.1 us
    dot_general x1, matrix products, shards(): jnp.dot(picked, proj_weight, preferred_element_type=jnp.float32)  9.55 us
    dot_general x1, matrix products, shards(): jnp.dot(placing, summed, preferred_element_type=jnp.float32)  7.41 us
    unnamed x1, waiting for transfers between devices  6.01 us
    all_to_all x1, starting transfers between devices, shards(): lax.all_to_all(outgoing, 'seq', split_axis=0, concat_axis=0, tiled=True)  5.2 us
    all_to_all x1, waiting for transfers between devices, shards(): lax.all_to_all(outgoing, 'seq', split_axis=0, concat_axis=0, tiled=True)  4.82 us
    unnamed x3, local copies, waits for them, and re-layouts  2.24 us
  transfers between devices with their start and end apart: 2, of which 2 were waited for; matrix products, arithmetic and copies ran while one was open for 3% of the time, Pallas kernels for 0%

commit v1 on v0

v1 whole, which is shorter than its diff:
```python
import functools

import jax
import jax.numpy as jnp
from jax import lax
from jax.experimental import pallas as pl
from jax.experimental.pallas import tpu as pltpu
from jax.sharding import PartitionSpec as P

CLIP_C = 1024
CNX_C = 3072
SIDE = 24
MESH = pl.DeviceIdType.MESH
CHUNK = 512


def up(value, unit):
    return -(-value // unit) * unit


def iota(shape, dim):
    return lax.broadcasted_iota(jnp.int32, shape, dim)


def floor_div(value, unit):
    return ((value.astype(jnp.float32) + 0.5) * (1.0 / unit)).astype(jnp.int32)


def to_row(column):
    size = column.shape[0]
    eye = iota((size, size), 0) == iota((size, size), 1)
    return jnp.sum(jnp.where(eye, column, 0), axis=0, keepdims=True)


def to_column(row):
    size = row.shape[1]
    eye = iota((size, size), 0) == iota((size, size), 1)
    return jnp.sum(jnp.where(eye, row, 0), axis=1, keepdims=True)


class Plan:
    def __init__(self, n_seq, n_tp, rows, width, depth, rows_here):
        self.n_seq, self.n_tp, self.rows, self.width = n_seq, n_tp, rows, width
        self.depth, self.rows_here = depth, rows_here
        self.cap = -(-rows // n_seq)
        self.cap_pad = up(self.cap, 16)
        self.slots = n_seq * self.cap_pad
        self.sub_cap = -(-(n_seq * self.cap) // n_tp)
        self.packed = up(n_tp * self.sub_cap, 8)
        self.groups = self.packed // 8
        self.chunks = depth // CHUNK
        self.first = [self.sub_cap * t // 8 for t in range(n_tp)]
        self.last = [-(-self.sub_cap * (t + 1) // 8) for t in range(n_tp)]
        self.window = max(b - a for a, b in zip(self.first, self.last))

    def right(self, t):
        return self.first[t + 1], self.groups

    def left(self, t):
        return 0, self.last[t - 1]


def join_kernel(
    plan, pos_ref, logit_ref, feat_ref, w_ref,
    out_ref, row_ref,
    wbuf, outgoing, arrived, picked, part, send_r, send_l, recv_r, recv_l,
    w_sem, x_send, x_recv, rs_send, rs_recv, ls_send, ls_recv,
):
    n_seq, n_tp, rows = plan.n_seq, plan.n_tp, plan.rows
    s = lax.axis_index("seq")
    t = lax.axis_index("tp")

    barrier = pltpu.get_barrier_semaphore()
    for step in range(1, n_seq):
        pl.semaphore_signal(barrier, inc=1, device_id={"seq": lax.rem(s + step, n_seq)}, device_id_type=MESH)

    @pl.when(t > 0)
    def _():
        pl.semaphore_signal(barrier, inc=1, device_id={"tp": t - 1}, device_id_type=MESH)

    @pl.when(t < n_tp - 1)
    def _():
        pl.semaphore_signal(barrier, inc=1, device_id={"tp": t + 1}, device_id_type=MESH)

    def weight_copy(k):
        return pltpu.make_async_copy(
            w_ref.at[:, pl.ds(pl.multiple_of(k * CHUNK, CHUNK), CHUNK)], wbuf.at[k], w_sem.at[k]
        )

    @pl.loop(0, plan.chunks)
    def _(k):
        weight_copy(k).start()

    row_id = s * rows + iota((rows, 1), 0)
    gates = []
    for encoder in range(3):
        picked_logit = jnp.zeros((rows, 1), jnp.float32)
        for image in range(logit_ref.shape[0]):
            here = (row_id >= image * SIDE * SIDE) & (row_id < (image + 1) * SIDE * SIDE)
            picked_logit = jnp.where(here, logit_ref[image, encoder], picked_logit)
        gates.append(jax.nn.sigmoid(picked_logit))
    channel = t * plan.width + iota((rows, plan.width), 1)
    gate = jnp.where(channel < CLIP_C, gates[0], jnp.where(channel < CLIP_C + CNX_C, gates[1], gates[2]))
    gated = (feat_ref[...].astype(jnp.float32) * gate).astype(jnp.bfloat16)

    seq_rows = plan.rows_here * n_tp
    own_pos = pos_ref[pl.ds(s, 1), :]
    own_target = floor_div(own_pos, seq_rows)
    target_col = to_column(own_target)
    before = iota((rows, rows), 0) < iota((rows, rows), 1)
    own_slot = jnp.sum(
        jnp.where((target_col == own_target) & before, 1, 0), axis=0, keepdims=True
    )
    address = own_target * plan.cap_pad + own_slot
    choose = (address == iota((plan.slots, rows), 0)).astype(jnp.float32).astype(jnp.bfloat16)
    outgoing[...] = (
        jnp.dot(choose, gated, preferred_element_type=jnp.float32)
        .astype(jnp.bfloat16)
        .reshape(n_seq, plan.cap_pad, plan.width)
    )

    neighbours = jnp.where(t > 0, 1, 0) + jnp.where(t < n_tp - 1, 1, 0)
    pl.semaphore_wait(barrier, n_seq - 1 + neighbours)

    def exchange(step):
        peer = lax.rem(s + step, n_seq)
        return pltpu.make_async_remote_copy(
            src_ref=outgoing.at[peer],
            dst_ref=arrived.at[s],
            send_sem=x_send.at[step],
            recv_sem=x_recv.at[step],
            device_id={"seq": peer},
            device_id_type=MESH,
        )

    for step in range(1, n_seq):
        exchange(step).start()
    arrived[s] = outgoing[s]

    positions = pos_ref[...]
    offset = positions - s * seq_rows
    here = (offset >= 0) & (offset < seq_rows)
    earlier = before.astype(jnp.float32).astype(jnp.bfloat16)
    count = jnp.dot(
        here.astype(jnp.float32).astype(jnp.bfloat16), earlier, preferred_element_type=jnp.float32
    ).astype(jnp.int32)
    count = jnp.where(here, count, -1)
    slot_shape = (n_seq, plan.cap_pad, rows)
    hit = count.reshape(n_seq, 1, rows) == iota(slot_shape, 1)
    offset_of = jnp.where(hit, offset.reshape(n_seq, 1, rows) + 1, 0).reshape(plan.slots, rows)
    offset_col = jnp.sum(offset_of, axis=1, keepdims=True) - 1
    valid_col = offset_col >= 0
    sub_col = jnp.where(valid_col, floor_div(offset_col, plan.rows_here), -1)
    sub_row = to_row(sub_col)
    offset_row = to_row(offset_col)
    square = (plan.slots, plan.slots)
    rank_row = jnp.sum(
        jnp.where((sub_col == sub_row) & (iota(square, 0) < iota(square, 1)), 1, 0), axis=0, keepdims=True
    )
    packed_row = jnp.where(sub_row >= 0, sub_row * plan.sub_cap + rank_row, -1)
    picking = (
        (packed_row == iota((plan.packed, plan.slots), 0)).astype(jnp.float32).astype(jnp.bfloat16)
    )
    window = plan.window * 8
    base = lax.div(plan.sub_cap * t, 8) * 8
    mine = (packed_row == base + iota((window, plan.slots), 0)) & (sub_row == t)
    local = jnp.sum(
        jnp.where(mine, offset_row - t * plan.rows_here + 1, 0), axis=1, keepdims=True
    ) - 1
    row_ref[...] = jnp.broadcast_to(local, row_ref.shape)

    for step in range(1, n_seq):
        exchange(step).wait_recv()
    picked[...] = jnp.dot(
        picking, arrived[...].reshape(plan.slots, plan.width), preferred_element_type=jnp.float32
    ).astype(jnp.bfloat16)

    def send_right(k, i):
        lo, hi = plan.right(i)
        return pltpu.make_async_remote_copy(
            src_ref=send_r.at[k, pl.ds(lo, hi - lo)],
            dst_ref=recv_r.at[k, pl.ds(lo, hi - lo)],
            send_sem=rs_send.at[k],
            recv_sem=rs_recv.at[k],
            device_id={"tp": lax.rem(t + 1, n_tp)},
            device_id_type=MESH,
        )

    def send_left(k, i):
        lo, hi = plan.left(i)
        return pltpu.make_async_remote_copy(
            src_ref=send_l.at[k, pl.ds(lo, hi - lo)],
            dst_ref=recv_l.at[k, pl.ds(lo, hi - lo)],
            send_sem=ls_send.at[k],
            recv_sem=ls_recv.at[k],
            device_id={"tp": lax.rem(t + n_tp - 1, n_tp)},
            device_id_type=MESH,
        )

    @pl.loop(0, plan.chunks)
    def _(k):
        weight_copy(k).wait()
        result = jnp.dot(picked[...], wbuf[k], preferred_element_type=jnp.float32)
        result = result.reshape(plan.groups, 8, CHUNK)
        part[k] = result

        @pl.when(t == 0)
        def _():
            lo, hi = plan.right(0)
            send_r[k, lo:hi] = result[lo:hi].astype(jnp.bfloat16)
            send_right(k, 0).start()

        @pl.when(t == n_tp - 1)
        def _():
            lo, hi = plan.left(n_tp - 1)
            send_l[k, lo:hi] = result[lo:hi].astype(jnp.bfloat16)
            send_left(k, n_tp - 1).start()

    for i in range(n_tp):

        @pl.when(t == i)
        def _(i=i):
            first, last = plan.first[i], plan.last[i]

            @pl.loop(0, plan.chunks)
            def _(k):
                total = part[k, first:last]
                if i > 0:
                    send_right(k, i - 1).wait_recv()
                    if i < n_tp - 1:
                        lo, hi = plan.right(i)
                        send_r[k, lo:hi] = (
                            part[k, lo:hi] + recv_r[k, lo:hi].astype(jnp.float32)
                        ).astype(jnp.bfloat16)
                        send_right(k, i).start()
                    total = total + recv_r[k, first:last].astype(jnp.float32)
                if i < n_tp - 1:
                    send_left(k, i + 1).wait_recv()
                    if i > 0:
                        lo, hi = plan.left(i)
                        send_l[k, lo:hi] = (
                            part[k, lo:hi] + recv_l[k, lo:hi].astype(jnp.float32)
                        ).astype(jnp.bfloat16)
                        send_left(k, i).start()
                    total = total + recv_l[k, first:last].astype(jnp.float32)
                columns = pl.ds(pl.multiple_of(k * CHUNK, CHUNK), CHUNK)
                out_ref[0 : last - first, :, columns] = total.astype(jnp.bfloat16)
                if last - first < plan.window:
                    out_ref[last - first :, :, columns] = jnp.zeros(
                        (plan.window - (last - first), 8, CHUNK), jnp.bfloat16
                    )

            @pl.loop(0, plan.chunks)
            def _(k):
                if i < n_tp - 1:
                    send_right(k, i).wait_send()
                if i > 0:
                    send_left(k, i).wait_send()

    for step in range(1, n_seq):
        exchange(step).wait_send()


def place_kernel(row_ref, summed_ref, text_ref, out_ref):
    block = text_ref.shape[0]
    window = summed_ref.shape[0] * 8
    local = row_ref[0:1, :] - pl.program_id(0) * block
    hits = (local == iota((block, window), 0)).astype(jnp.float32)
    filled = jnp.sum(hits, axis=1, keepdims=True) > 0.5
    values = summed_ref[...].reshape(window, text_ref.shape[1])
    placed = jnp.dot(hits.astype(jnp.bfloat16), values, preferred_element_type=jnp.float32)
    out_ref[...] = jnp.where(filled, placed.astype(jnp.bfloat16), text_ref[...])


def shards(features, gate_logits, proj_weight, positions, text):
    n_seq, n_tp = lax.axis_size("seq"), lax.axis_size("tp")
    rows, width = features.shape
    depth = proj_weight.shape[1]
    rows_here = text.shape[0]
    plan = Plan(n_seq, n_tp, rows, width, depth, rows_here)
    vmem = pl.BlockSpec(memory_space=pltpu.VMEM)
    moving = pltpu.VMEM((plan.chunks, plan.groups, 8, CHUNK), jnp.bfloat16)
    summed, local_rows = pl.pallas_call(
        functools.partial(join_kernel, plan),
        out_shape=(
            jax.ShapeDtypeStruct((plan.window, 8, depth), jnp.bfloat16),
            jax.ShapeDtypeStruct((plan.window * 8, 128), jnp.int32),
        ),
        in_specs=[
            vmem,
            pl.BlockSpec(memory_space=pltpu.SMEM),
            vmem,
            pl.BlockSpec(memory_space=pl.ANY),
        ],
        out_specs=(vmem, vmem),
        scratch_shapes=[
            pltpu.VMEM((plan.chunks, width, CHUNK), jnp.bfloat16),
            pltpu.VMEM((n_seq, plan.cap_pad, width), jnp.bfloat16),
            pltpu.VMEM((n_seq, plan.cap_pad, width), jnp.bfloat16),
            pltpu.VMEM((plan.packed, width), jnp.bfloat16),
            pltpu.VMEM((plan.chunks, plan.groups, 8, CHUNK), jnp.float32),
            moving, moving, moving, moving,
            pltpu.SemaphoreType.DMA((plan.chunks,)),
            pltpu.SemaphoreType.DMA((n_seq,)),
            pltpu.SemaphoreType.DMA((n_seq,)),
            pltpu.SemaphoreType.DMA((plan.chunks,)),
            pltpu.SemaphoreType.DMA((plan.chunks,)),
            pltpu.SemaphoreType.DMA((plan.chunks,)),
            pltpu.SemaphoreType.DMA((plan.chunks,)),
        ],
        compiler_params=pltpu.CompilerParams(collective_id=0, has_side_effects=True),
        name="join",
    )(positions.reshape(n_seq, rows), gate_logits, features, proj_weight)

    window = plan.window * 8
    local_rows = local_rows[:, 0].reshape(1, window)
    block = 64 if rows_here % 64 == 0 else rows_here
    return pl.pallas_call(
        place_kernel,
        grid=(rows_here // block,),
        out_shape=jax.ShapeDtypeStruct(text.shape, text.dtype),
        in_specs=[
            pl.BlockSpec((1, window), lambda i: (0, 0)),
            pl.BlockSpec((plan.window, 8, depth), lambda i: (0, 0, 0)),
            pl.BlockSpec((block, depth), lambda i: (i, 0)),
        ],
        out_specs=pl.BlockSpec((block, depth), lambda i: (i, 0)),
        compiler_params=pltpu.CompilerParams(vmem_limit_bytes=24 * 1024 * 1024),
        name="place",
    )(local_rows, summed, text)


def solution(mesh):
    return jax.shard_map(
        shards,
        mesh=mesh,
        in_specs=(P("seq", "tp"), P(), P("tp", None), P(), P(("seq", "tp"), None)),
        out_specs=P(("seq", "tp"), None),
        check_vma=False,
    )
```

time: 77.3 us -> 130 us (1.68)
  Pallas kernels: 0 us -> 123 us
  blocking collectives: 33.1 us -> 0 us
  matrix products: 18.2 us -> 0 us
  waiting for transfers between devices: 10.8 us -> 0 us
  starting transfers between devices: 6.51 us -> 0 us
  other arithmetic: 2.51 us -> 0 us
  local copies, waits for them, and re-layouts: 3.75 us -> 5.95 us
    pallas_call x0 -> x2, Pallas kernels: none -> 123 us  [the longest x1 119 us: shards(): pl.pallas_call(functools.partial(join_kernel, plan), out_shape=(jax.Shape...]
    unnamed x1 -> x0, blocking collectives: 33.1 us -> none
    dot_general x3 -> x0, matrix products: 18.2 us -> none  [the longest x1 9.55 us: shards(): jnp.dot(picked, proj_weight, preferred_element_type=jnp.float32)]
    unnamed x1 -> x0, waiting for transfers between devices: 6.01 us -> none
    all_to_all x1 -> x0, starting transfers between devices: 5.2 us -> none  [shards(): lax.all_to_all(outgoing, 'seq', split_axis=0, concat_axis=0, tiled=True)]
    all_to_all x1 -> x0, waiting for transfers between devices: 4.82 us -> none  [shards(): lax.all_to_all(outgoing, 'seq', split_axis=0, concat_axis=0, tiled=True)]
    unnamed x3 -> x4, local copies, waits for them, and re-layouts: 2.24 us -> 3.78 us
    reshape x0 -> x1, local copies, waits for them, and re-layouts: none -> 1.35 us  [shards(): positions.reshape(n_seq, rows)]
  transfers between devices with their start and end apart: 2 -> 0, of which waited for: 2 -> 0; matrix products, arithmetic and copies ran while one was open for 3% -> 0% of each run, Pallas kernels for 0% -> 0%
where the time goes in v1:
time: 130 us; the launch traced here: 129 us
  Pallas kernels  123 us (95%)
  local copies, waits for them, and re-layouts  5.95 us (5%)
    pallas_call x1, Pallas kernels, shards(): pl.pallas_call(functools.partial(join_kernel, plan), out_shape=(jax.Shape...  119 us
    pallas_call x1, Pallas kernels, shards(): pl.pallas_call(place_kernel, grid=(rows_here // block,), out_shape=jax.Sh...  4.56 us
    unnamed x4, local copies, waits for them, and re-layouts  3.78 us

profile of v1, /device:TPU:0, one launch (start us, length us, event | category | flops | bytes accessed | tf_op | source)
XLA Modules:
  0.0 129.3 jit_solution(14332097239710391855)
XLA Ops:
  0.0 1.4 %reshape.3.pos_ref = s32[8,72]{1,0:T(8,128)} reshape(s32[576]{0:T(1024)} %param.8) | data formatting | bytes 4608 | tf_op jit(solution)/shard_map/reshape | solution.py:313
  1.4 118.8 %join.1 = (bf16[3,8,8192]{2,1,0:T(8,128)(2,1)}, s32[24,128]{1,0:T(8,128)}) custom-call(s32[8,72]{1,0:T(8,128)} %reshape.3.pos_ref, f32[1,3]{1,0:T(1,128)} %logit_ref.1, bf16[72,1344]{1,0:T(8,128)(2,1)} %feat_ref.1, bf16[1344,8192]{1,0:T(8,128)(2,1)} %w_ref.1), custom_call_target="tpu_custom_call" | custom-call | tf_op jit(solution)/shard_map/join/pallas_call | solution.py:283
  120.1 0.8 slice_reduce_fusion
  121.0 0.0 copy-start
  121.0 2.8 %copy-done = bf16[384,8192]{1,0:T(8,128)(2,1)S(1)} copy-done((bf16[384,8192]{1,0:T(8,128)(2,1)S(1)}, bf16[384,8192]{1,0:T(8,128)(2,1)}, u32[]{:S(2)}) %copy-start) | copy-done | bytes 6291480
  123.8 0.0 copy-start.1
  123.8 1.0 copy-done.1
  124.8 4.6 %place.1 = bf16[384,8192]{1,0:T(8,128)(2,1)} custom-call(s32[1,24]{1,0:T(1,128)S(1)} %bitcast.1, bf16[3,8,8192]{2,1,0:T(8,128)(2,1)S(1)} %copy-done.1, bf16[384,8192]{1,0:T(8,128)(2,1)S(1)} %copy-done), custom_call_target="tpu_custom_call" | custom-call | tf_op jit(solution)/shard_map/place/pallas_call | solution.py:318
Async XLA Ops:
  121.0 2.8 %copy-start = (bf16[384,8192]{1,0:T(8,128)(2,1)S(1)}, bf16[384,8192]{1,0:T(8,128)(2,1)}, u32[]{:S(2)}) copy-start(bf16[384,8192]{1,0:T(8,128)(2,1)} %text_ref.1) | copy-start | bytes 18874372
  123.8 1.0 copy-start.1

commit v2 on v1

--- a/solution.py
+++ b/solution.py
@@ -12,6 +12,7 @@
 SIDE = 24
 MESH = pl.DeviceIdType.MESH
 CHUNK = 512
+LAG = 6
 
 
 def up(value, unit):
@@ -61,9 +62,9 @@
 
 
 def join_kernel(
-    plan, pos_ref, logit_ref, feat_ref, w_ref,
+    plan, flat_ref, logit_ref, feat_ref, w_ref,
     out_ref, row_ref,
-    wbuf, outgoing, arrived, picked, part, send_r, send_l, recv_r, recv_l,
+    pos_ref, wbuf, outgoing, arrived, picked, part, send_r, send_l, recv_r, recv_l,
     w_sem, x_send, x_recv, rs_send, rs_recv, ls_send, ls_recv,
 ):
     n_seq, n_tp, rows = plan.n_seq, plan.n_tp, plan.rows
@@ -90,6 +91,9 @@
     @pl.loop(0, plan.chunks)
     def _(k):
         weight_copy(k).start()
+
+    for source in range(n_seq):
+        pos_ref[source : source + 1, :] = flat_ref[:, source * rows : (source + 1) * rows]
 
     row_id = s * rows + iota((rows, 1), 0)
     gates = []
@@ -167,7 +171,7 @@
     local = jnp.sum(
         jnp.where(mine, offset_row - t * plan.rows_here + 1, 0), axis=1, keepdims=True
     ) - 1
-    row_ref[...] = jnp.broadcast_to(local, row_ref.shape)
+    row_ref[...] = to_row(local)
 
     for step in range(1, n_seq):
         exchange(step).wait_recv()
@@ -197,59 +201,68 @@
             device_id_type=MESH,
         )
 
-    @pl.loop(0, plan.chunks)
-    def _(k):
-        weight_copy(k).wait()
-        result = jnp.dot(picked[...], wbuf[k], preferred_element_type=jnp.float32)
-        result = result.reshape(plan.groups, 8, CHUNK)
-        part[k] = result
-
-        @pl.when(t == 0)
+    def pass_right(k, i):
+        if i > 0:
+            send_right(k, i - 1).wait_recv()
+        if i < n_tp - 1:
+            lo, hi = plan.right(i)
+            block = part[k, lo:hi]
+            if i > 0:
+                block = block + recv_r[k, lo:hi].astype(jnp.float32)
+            send_r[k, lo:hi] = block.astype(jnp.bfloat16)
+            send_right(k, i).start()
+
+    def pass_left(k, i):
+        if i < n_tp - 1:
+            send_left(k, i + 1).wait_recv()
+        if i > 0:
+            lo, hi = plan.left(i)
+            block = part[k, lo:hi]
+            if i < n_tp - 1:
+                block = block + recv_l[k, lo:hi].astype(jnp.float32)
+            send_l[k, lo:hi] = block.astype(jnp.bfloat16)
+            send_left(k, i).start()
+
+    def finish(k, i):
+        first, last = plan.first[i], plan.last[i]
+        total = part[k, first:last]
+        if i > 0:
+            total = total + recv_r[k, first:last].astype(jnp.float32)
+        if i < n_tp - 1:
+            total = total + recv_l[k, first:last].astype(jnp.float32)
+        columns = pl.ds(pl.multiple_of(k * CHUNK, CHUNK), CHUNK)
+        out_ref[0 : last - first, :, columns] = total.astype(jnp.bfloat16)
+        if last - first < plan.window:
+            out_ref[last - first :, :, columns] = jnp.zeros(
+                (plan.window - (last - first), 8, CHUNK), jnp.bfloat16
+            )
+
+    lags = [min(LAG * (abs(2 * i - n_tp + 1) + 1) // 2, plan.chunks) for i in range(n_tp)]
+
+    @pl.loop(0, plan.chunks + max(lags))
+    def _(step):
+        @pl.when(step < plan.chunks)
         def _():
-            lo, hi = plan.right(0)
-            send_r[k, lo:hi] = result[lo:hi].astype(jnp.bfloat16)
-            send_right(k, 0).start()
-
-        @pl.when(t == n_tp - 1)
-        def _():
-            lo, hi = plan.left(n_tp - 1)
-            send_l[k, lo:hi] = result[lo:hi].astype(jnp.bfloat16)
-            send_left(k, n_tp - 1).start()
+            weight_copy(step).wait()
+            result = jnp.dot(picked[...], wbuf[step], preferred_element_type=jnp.float32)
+            part[step] = result.reshape(plan.groups, 8, CHUNK)
+            for i in range(n_tp):
+
+                @pl.when(t == i)
+                def _(i=i):
+                    (pass_right if 2 * i < n_tp else pass_left)(step, i)
+
+        for i in range(n_tp):
+
+            @pl.when((t == i) & (step >= lags[i]) & (step < plan.chunks + lags[i]))
+            def _(i=i):
+                (pass_left if 2 * i < n_tp else pass_right)(step - lags[i], i)
+                finish(step - lags[i], i)
 
     for i in range(n_tp):
 
         @pl.when(t == i)
         def _(i=i):
-            first, last = plan.first[i], plan.last[i]
-
-            @pl.loop(0, plan.chunks)
-            def _(k):
-                total = part[k, first:last]
-                if i > 0:
-                    send_right(k, i - 1).wait_recv()
-                    if i < n_tp - 1:
-                        lo, hi = plan.right(i)
-                        send_r[k, lo:hi] = (
-                            part[k, lo:hi] + recv_r[k, lo:hi].astype(jnp.float32)
-                        ).astype(jnp.bfloat16)
-                        send_right(k, i).start()
-                    total = total + recv_r[k, first:last].astype(jnp.float32)
-                if i < n_tp - 1:
-                    send_left(k, i + 1).wait_recv()
-                    if i > 0:
-                        lo, hi = plan.left(i)
-                        send_l[k, lo:hi] = (
-                            part[k, lo:hi] + recv_l[k, lo:hi].astype(jnp.float32)
-                        ).astype(jnp.bfloat16)
-                        send_left(k, i).start()
-                    total = total + recv_l[k, first:last].astype(jnp.float32)
-                columns = pl.ds(pl.multiple_of(k * CHUNK, CHUNK), CHUNK)
-                out_ref[0 : last - first, :, columns] = total.astype(jnp.bfloat16)
-                if last - first < plan.window:
-                    out_ref[last - first :, :, columns] = jnp.zeros(
-                        (plan.window - (last - first), 8, CHUNK), jnp.bfloat16
-                    )
-
             @pl.loop(0, plan.chunks)
             def _(k):
                 if i < n_tp - 1:
@@ -284,7 +297,7 @@
         functools.partial(join_kernel, plan),
         out_shape=(
             jax.ShapeDtypeStruct((plan.window, 8, depth), jnp.bfloat16),
-            jax.ShapeDtypeStruct((plan.window * 8, 128), jnp.int32),
+            jax.ShapeDtypeStruct((1, plan.window * 8), jnp.int32),
         ),
         in_specs=[
             vmem,
@@ -294,6 +307,7 @@
         ],
         out_specs=(vmem, vmem),
         scratch_shapes=[
+            pltpu.VMEM((n_seq, rows), jnp.int32),
             pltpu.VMEM((plan.chunks, width, CHUNK), jnp.bfloat16),
             pltpu.VMEM((n_seq, plan.cap_pad, width), jnp.bfloat16),
             pltpu.VMEM((n_seq, plan.cap_pad, width), jnp.bfloat16),
@@ -308,12 +322,13 @@
             pltpu.SemaphoreType.DMA((plan.chunks,)),
             pltpu.SemaphoreType.DMA((plan.chunks,)),
         ],
-        compiler_params=pltpu.CompilerParams(collective_id=0, has_side_effects=True),
+        compiler_params=pltpu.CompilerParams(
+            collective_id=0, has_side_effects=True, vmem_limit_bytes=44 * 1024 * 1024
+        ),
         name="join",
-    )(positions.reshape(n_seq, rows), gate_logits, features, proj_weight)
+    )(positions.reshape(1, n_seq * rows), gate_logits, features, proj_weight)
 
     window = plan.window * 8
-    local_rows = local_rows[:, 0].reshape(1, window)
     block = 64 if rows_here % 64 == 0 else rows_here
     return pl.pallas_call(
         place_kernel,

time: 130 us -> 47.5 us (0.37)
  Pallas kernels: 123 us -> 45 us
  local copies, waits for them, and re-layouts: 5.95 us -> 2.28 us
    pallas_call x1, Pallas kernels: 119 us -> 40.4 us  [shards(): pl.pallas_call(functools.partial(join_kernel, plan), out_shape=(jax.Shape...]
    unnamed x4 -> x6, local copies, waits for them, and re-layouts: 3.78 us -> 1.59 us
where the time goes in v2:
time: 47.5 us; the launch traced here: 47.3 us
  Pallas kernels  45 us (95%)
  local copies, waits for them, and re-layouts  2.28 us (5%)
    pallas_call x1, Pallas kernels, shards(): pl.pallas_call(functools.partial(join_kernel, plan), out_shape=(jax.Shape...  40.4 us
    pallas_call x1, Pallas kernels, shards(): pl.pallas_call(place_kernel, grid=(rows_here // block,), out_shape=jax.Sh...  4.59 us
    unnamed x6, local copies, waits for them, and re-layouts  1.59 us

profile of v2, /device:TPU:0, one launch (start us, length us, event | category | flops | bytes accessed | tf_op | source)
XLA Modules:
  0.0 47.3 jit_solution(15477615875470724657)
XLA Ops:
  0.0 0.7 %reshape.3.flat_ref = s32[1,576]{1,0:T(1,128)S(1)} reshape(s32[576]{0:T(1024)} %param.8) | data formatting | bytes 4608 | tf_op jit(solution)/shard_map/reshape | solution.py:329
  0.7 0.0 copy-start.1
  0.7 0.9 %copy-done.1 = bf16[72,1344]{1,0:T(8,128)(2,1)S(1)} copy-done((bf16[72,1344]{1,0:T(8,128)(2,1)S(1)}, bf16[72,1344]{1,0:T(8,128)(2,1)}, u32[]{:S(2)}) %copy-start.1) | copy-done | bytes 193560
  1.6 0.0 copy-start.2
  1.6 0.7 %copy-done.2 = f32[1,3]{1,0:T(1,128)S(1)} copy-done((f32[1,3]{1,0:T(1,128)S(1)}, f32[1,3]{1,0:T(1,128)}, u32[]{:S(2)}) %copy-start.2) | copy-done | bytes 36
  2.3 0.0 copy-start
  2.3 40.4 %join.1 = (bf16[3,8,8192]{2,1,0:T(8,128)(2,1)S(1)}, s32[1,24]{1,0:T(1,128)S(1)}) custom-call(s32[1,576]{1,0:T(1,128)S(1)} %reshape.3.flat_ref, f32[1,3]{1,0:T(1,128)S(1)} %copy-done.2, bf16[72,1344]{1,0:T(8,128)(2,1)S(1)} %copy-done.1, bf16[1344,8192]{1,0:T(8,128)(2,1)} %w_ref.1), custom_call_target="tpu_custom_call" | custom-call | tf_op jit(solution)/shard_map/join/pallas_call | solution.py:296
  42.7 0.0 copy-done
  42.7 4.6 %place.1 = bf16[384,8192]{1,0:T(8,128)(2,1)} custom-call(s32[1,24]{1,0:T(1,128)S(1)} %get-tuple-element.7.row_ref, bf16[3,8,8192]{2,1,0:T(8,128)(2,1)S(1)} %get-tuple-element.8.summed_ref, bf16[384,8192]{1,0:T(8,128)(2,1)S(1)} %copy-done), custom_call_target="tpu_custom_call" | custom-call | tf_op jit(solution)/shard_map/place/pallas_call | solution.py:333
Async XLA Ops:
  0.7 0.9 %copy-start.1 = (bf16[72,1344]{1,0:T(8,128)(2,1)S(1)}, bf16[72,1344]{1,0:T(8,128)(2,1)}, u32[]{:S(2)}) copy-start(bf16[72,1344]{1,0:T(8,128)(2,1)} %feat_ref.1) | copy-start | bytes 580612
  1.6 0.7 %copy-start.2 = (f32[1,3]{1,0:T(1,128)S(1)}, f32[1,3]{1,0:T(1,128)}, u32[]{:S(2)}) copy-start(f32[1,3]{1,0:T(1,128)} %logit_ref.1) | copy-start | bytes 40
  2.3 40.4 %copy-start = (bf16[384,8192]{1,0:T(8,128)(2,1)S(1)}, bf16[384,8192]{1,0:T(8,128)(2,1)}, u32[]{:S(2)}) copy-start(bf16[384,8192]{1,0:T(8,128)(2,1)} %text_ref.1) | copy-start | bytes 18874372

commit v3 on v2

--- a/solution.py
+++ b/solution.py
@@ -11,8 +11,8 @@
 CNX_C = 3072
 SIDE = 24
 MESH = pl.DeviceIdType.MESH
-CHUNK = 512
-LAG = 6
+CHUNK = 1024
+LAG = 4
 
 
 def up(value, unit):
@@ -54,11 +54,11 @@
         self.last = [-(-self.sub_cap * (t + 1) // 8) for t in range(n_tp)]
         self.window = max(b - a for a, b in zip(self.first, self.last))
 
-    def right(self, t):
-        return self.first[t + 1], self.groups
-
-    def left(self, t):
-        return 0, self.last[t - 1]
+    def right(self, dest):
+        return self.first[dest], self.first[dest + 1] if dest < self.n_tp - 1 else self.groups
+
+    def left(self, dest):
+        return self.last[dest - 1] if dest > 0 else 0, self.last[dest]
 
 
 def join_kernel(
@@ -179,51 +179,59 @@
         picking, arrived[...].reshape(plan.slots, plan.width), preferred_element_type=jnp.float32
     ).astype(jnp.bfloat16)
 
-    def send_right(k, i):
-        lo, hi = plan.right(i)
+    chunks = plan.chunks
+
+    def send_right(k, dest):
+        lo, hi = plan.right(dest)
         return pltpu.make_async_remote_copy(
             src_ref=send_r.at[k, pl.ds(lo, hi - lo)],
             dst_ref=recv_r.at[k, pl.ds(lo, hi - lo)],
-            send_sem=rs_send.at[k],
-            recv_sem=rs_recv.at[k],
+            send_sem=rs_send.at[dest * chunks + k],
+            recv_sem=rs_recv.at[dest * chunks + k],
             device_id={"tp": lax.rem(t + 1, n_tp)},
             device_id_type=MESH,
         )
 
-    def send_left(k, i):
-        lo, hi = plan.left(i)
+    def send_left(k, dest):
+        lo, hi = plan.left(dest)
         return pltpu.make_async_remote_copy(
             src_ref=send_l.at[k, pl.ds(lo, hi - lo)],
             dst_ref=recv_l.at[k, pl.ds(lo, hi - lo)],
-            send_sem=ls_send.at[k],
-            recv_sem=ls_recv.at[k],
+            send_sem=ls_send.at[dest * chunks + k],
+            recv_sem=ls_recv.at[dest * chunks + k],
             device_id={"tp": lax.rem(t + n_tp - 1, n_tp)},
             device_id_type=MESH,
         )
 
-    def pass_right(k, i):
+    def pass_right(i, phase, k):
+        dest = n_tp - 1 - phase
+        if dest < i:
+            return
         if i > 0:
-            send_right(k, i - 1).wait_recv()
-        if i < n_tp - 1:
-            lo, hi = plan.right(i)
+            send_right(k, dest).wait_recv()
+        if dest > i:
+            lo, hi = plan.right(dest)
             block = part[k, lo:hi]
             if i > 0:
                 block = block + recv_r[k, lo:hi].astype(jnp.float32)
             send_r[k, lo:hi] = block.astype(jnp.bfloat16)
-            send_right(k, i).start()
-
-    def pass_left(k, i):
+            send_right(k, dest).start()
+
+    def pass_left(i, phase, k):
+        dest = phase
+        if dest > i:
+            return
         if i < n_tp - 1:
-            send_left(k, i + 1).wait_recv()
-        if i > 0:
-            lo, hi = plan.left(i)
+            send_left(k, dest).wait_recv()
+        if dest < i:
+            lo, hi = plan.left(dest)
             block = part[k, lo:hi]
             if i < n_tp - 1:
                 block = block + recv_l[k, lo:hi].astype(jnp.float32)
             send_l[k, lo:hi] = block.astype(jnp.bfloat16)
-            send_left(k, i).start()
-
-    def finish(k, i):
+            send_left(k, dest).start()
+
+    def finish(i, phase, k):
         first, last = plan.first[i], plan.last[i]
         total = part[k, first:last]
         if i > 0:
@@ -237,38 +245,67 @@
                 (plan.window - (last - first), 8, CHUNK), jnp.bfloat16
             )
 
-    lags = [min(LAG * (abs(2 * i - n_tp + 1) + 1) // 2, plan.chunks) for i in range(n_tp)]
-
-    @pl.loop(0, plan.chunks + max(lags))
-    def _(step):
-        @pl.when(step < plan.chunks)
-        def _():
-            weight_copy(step).wait()
-            result = jnp.dot(picked[...], wbuf[step], preferred_element_type=jnp.float32)
-            part[step] = result.reshape(plan.groups, 8, CHUNK)
-            for i in range(n_tp):
-
-                @pl.when(t == i)
-                def _(i=i):
-                    (pass_right if 2 * i < n_tp else pass_left)(step, i)
-
+    def shifted(i, block, k, offset, count, act):
+        skip, part_of = divmod(offset, chunks)
+        phase = block - skip
+        if 0 <= phase < count:
+
+            @pl.when(k >= part_of)
+            def _():
+                act(i, phase, k - part_of)
+
+        if part_of > 0 and 0 <= phase - 1 < count:
+
+            @pl.when(k < part_of)
+            def _():
+                act(i, phase - 1, k - part_of + chunks)
+
+    def schedule(i):
+        near_right = 2 * i < n_tp
+        end = i in (0, n_tp - 1)
+        hops = (abs(2 * i - n_tp + 1) + 1) // 2
+        lag = (n_tp - 1) * chunks if end else min(LAG * hops, chunks)
+        right_last, left_last = n_tp - 1 - i, i
+        near_last, far_last = (right_last, left_last) if near_right else (left_last, right_last)
+        done = max(0 if end else near_last * chunks, far_last * chunks + lag)
+        return near_right, lag, far_last + 1, done
+
+    def block_step(i, block, k):
+        near_right, lag, far_count, done = schedule(i)
+        near, far = (pass_right, pass_left) if near_right else (pass_left, pass_right)
+        if block < n_tp:
+            near(i, block, k)
+        shifted(i, block, k, lag, far_count, far)
+        shifted(i, block, k, done, 1, finish)
+
+    @pl.loop(0, chunks)
+    def _(k):
+        weight_copy(k).wait()
+        result = jnp.dot(picked[...], wbuf[k], preferred_element_type=jnp.float32)
+        part[k] = result.reshape(plan.groups, 8, CHUNK)
         for i in range(n_tp):
 
-            @pl.when((t == i) & (step >= lags[i]) & (step < plan.chunks + lags[i]))
+            @pl.when(t == i)
             def _(i=i):
-                (pass_left if 2 * i < n_tp else pass_right)(step - lags[i], i)
-                finish(step - lags[i], i)
+                block_step(i, 0, k)
 
     for i in range(n_tp):
 
         @pl.when(t == i)
         def _(i=i):
-            @pl.loop(0, plan.chunks)
+            done = schedule(i)[3]
+            for block in range(1, -(-done // chunks) + 1):
+
+                @pl.loop(0, chunks)
+                def _(k):
+                    block_step(i, block, k)
+
+            @pl.loop(0, chunks)
             def _(k):
-                if i < n_tp - 1:
-                    send_right(k, i).wait_send()
-                if i > 0:
-                    send_left(k, i).wait_send()
+                for dest in range(i + 1, n_tp):
+                    send_right(k, dest).wait_send()
+                for dest in range(i):
+                    send_left(k, dest).wait_send()
 
     for step in range(1, n_seq):
         exchange(step).wait_send()
@@ -317,10 +354,10 @@
             pltpu.SemaphoreType.DMA((plan.chunks,)),
             pltpu.SemaphoreType.DMA((n_seq,)),
             pltpu.SemaphoreType.DMA((n_seq,)),
-            pltpu.SemaphoreType.DMA((plan.chunks,)),
-            pltpu.SemaphoreType.DMA((plan.chunks,)),
-            pltpu.SemaphoreType.DMA((plan.chunks,)),
-            pltpu.SemaphoreType.DMA((plan.chunks,)),
+            pltpu.SemaphoreType.DMA((n_tp * plan.chunks,)),
+            pltpu.SemaphoreType.DMA((n_tp * plan.chunks,)),
+            pltpu.SemaphoreType.DMA((n_tp * plan.chunks,)),
+            pltpu.SemaphoreType.DMA((n_tp * plan.chunks,)),
         ],
         compiler_params=pltpu.CompilerParams(
             collective_id=0, has_side_effects=True, vmem_limit_bytes=44 * 1024 * 1024

time: 47.5 us -> 39.9 us (0.84)
  the two profiles are of different devices: /device:TPU:0 before, /device:TPU:21 now
where the time goes in v3:
time: 39.9 us; the launch traced here: 39.7 us
  Pallas kernels  37.4 us (94%)
  local copies, waits for them, and re-layouts  2.28 us (6%)
    pallas_call x1, Pallas kernels, shards(): pl.pallas_call(functools.partial(join_kernel, plan), out_shape=(jax.Shape...  32.9 us
    pallas_call x1, Pallas kernels, shards(): pl.pallas_call(place_kernel, grid=(rows_here // block,), out_shape=jax.Sh...  4.59 us
    unnamed x6, local copies, waits for them, and re-layouts  1.59 us

profile of v3, /device:TPU:21, one launch (start us, length us, event | category | flops | bytes accessed | tf_op | source)
XLA Modules:
  0.0 39.7 jit_solution(72458472033220665)
XLA Ops:
  0.0 0.7 %reshape.3.flat_ref = s32[1,576]{1,0:T(1,128)S(1)} reshape(s32[576]{0:T(1024)} %param.8) | data formatting | bytes 4608 | tf_op jit(solution)/shard_map/reshape | solution.py:366
  0.7 0.0 copy-start.1
  0.7 0.9 %copy-done.1 = bf16[72,1344]{1,0:T(8,128)(2,1)S(1)} copy-done((bf16[72,1344]{1,0:T(8,128)(2,1)S(1)}, bf16[72,1344]{1,0:T(8,128)(2,1)}, u32[]{:S(2)}) %copy-start.1) | copy-done | bytes 193560
  1.6 0.0 copy-start.2
  1.6 0.7 %copy-done.2 = f32[1,3]{1,0:T(1,128)S(1)} copy-done((f32[1,3]{1,0:T(1,128)S(1)}, f32[1,3]{1,0:T(1,128)}, u32[]{:S(2)}) %copy-start.2) | copy-done | bytes 36
  2.3 0.0 copy-start
  2.3 32.9 %join.1 = (bf16[3,8,8192]{2,1,0:T(8,128)(2,1)S(1)}, s32[1,24]{1,0:T(1,128)S(1)}) custom-call(s32[1,576]{1,0:T(1,128)S(1)} %reshape.3.flat_ref, f32[1,3]{1,0:T(1,128)S(1)} %copy-done.2, bf16[72,1344]{1,0:T(8,128)(2,1)S(1)} %copy-done.1, bf16[1344,8192]{1,0:T(8,128)(2,1)} %w_ref.1), custom_call_target="tpu_custom_call" | custom-call | tf_op jit(solution)/shard_map/join/pallas_call | solution.py:333
  35.1 0.0 copy-done
  35.1 4.6 %place.1 = bf16[384,8192]{1,0:T(8,128)(2,1)} custom-call(s32[1,24]{1,0:T(1,128)S(1)} %get-tuple-element.7.row_ref, bf16[3,8,8192]{2,1,0:T(8,128)(2,1)S(1)} %get-tuple-element.8.summed_ref, bf16[384,8192]{1,0:T(8,128)(2,1)S(1)} %copy-done), custom_call_target="tpu_custom_call" | custom-call | tf_op jit(solution)/shard_map/place/pallas_call | solution.py:370
Async XLA Ops:
  0.7 0.9 %copy-start.1 = (bf16[72,1344]{1,0:T(8,128)(2,1)S(1)}, bf16[72,1344]{1,0:T(8,128)(2,1)}, u32[]{:S(2)}) copy-start(bf16[72,1344]{1,0:T(8,128)(2,1)} %feat_ref.1) | copy-start | bytes 580612
  1.6 0.7 %copy-start.2 = (f32[1,3]{1,0:T(1,128)S(1)}, f32[1,3]{1,0:T(1,128)}, u32[]{:S(2)}) copy-start(f32[1,3]{1,0:T(1,128)} %logit_ref.1) | copy-start | bytes 40
  2.3 32.9 %copy-start = (bf16[384,8192]{1,0:T(8,128)(2,1)S(1)}, bf16[384,8192]{1,0:T(8,128)(2,1)}, u32[]{:S(2)}) copy-start(bf16[384,8192]{1,0:T(8,128)(2,1)} %text_ref.1) | copy-start | bytes 18874372

commit v4 on v3

--- a/solution.py
+++ b/solution.py
@@ -62,15 +62,20 @@
 
 
 def join_kernel(
-    plan, flat_ref, logit_ref, feat_ref, w_ref,
+    plan, flat_ref, logit_hbm, feat_hbm, w_ref,
     out_ref, row_ref,
-    pos_ref, wbuf, outgoing, arrived, picked, part, send_r, send_l, recv_r, recv_l,
+    logit_ref, feat_ref, in_sem, pos_ref, wbuf, outgoing, arrived, picked, part, send_r, send_l, recv_r, recv_l,
     w_sem, x_send, x_recv, rs_send, rs_recv, ls_send, ls_recv,
 ):
     n_seq, n_tp, rows = plan.n_seq, plan.n_tp, plan.rows
     s = lax.axis_index("seq")
     t = lax.axis_index("tp")
 
+    feat_copy = pltpu.make_async_copy(feat_hbm, feat_ref, in_sem.at[0])
+    logit_copy = pltpu.make_async_copy(logit_hbm, logit_ref, in_sem.at[1])
+    feat_copy.start()
+    logit_copy.start()
+
     barrier = pltpu.get_barrier_semaphore()
     for step in range(1, n_seq):
         pl.semaphore_signal(barrier, inc=1, device_id={"seq": lax.rem(s + step, n_seq)}, device_id_type=MESH)
@@ -95,6 +100,19 @@
     for source in range(n_seq):
         pos_ref[source : source + 1, :] = flat_ref[:, source * rows : (source + 1) * rows]
 
+    seq_rows = plan.rows_here * n_tp
+    own_pos = pos_ref[pl.ds(s, 1), :]
+    own_target = floor_div(own_pos, seq_rows)
+    target_col = to_column(own_target)
+    before = iota((rows, rows), 0) < iota((rows, rows), 1)
+    own_slot = jnp.sum(
+        jnp.where((target_col == own_target) & before, 1, 0), axis=0, keepdims=True
+    )
+    address = own_target * plan.cap_pad + own_slot
+    choose = (address == iota((plan.slots, rows), 0)).astype(jnp.float32).astype(jnp.bfloat16)
+
+    logit_copy.wait()
+    feat_copy.wait()
     row_id = s * rows + iota((rows, 1), 0)
     gates = []
     for encoder in range(3):
@@ -106,17 +124,6 @@
     channel = t * plan.width + iota((rows, plan.width), 1)
     gate = jnp.where(channel < CLIP_C, gates[0], jnp.where(channel < CLIP_C + CNX_C, gates[1], gates[2]))
     gated = (feat_ref[...].astype(jnp.float32) * gate).astype(jnp.bfloat16)
-
-    seq_rows = plan.rows_here * n_tp
-    own_pos = pos_ref[pl.ds(s, 1), :]
-    own_target = floor_div(own_pos, seq_rows)
-    target_col = to_column(own_target)
-    before = iota((rows, rows), 0) < iota((rows, rows), 1)
-    own_slot = jnp.sum(
-        jnp.where((target_col == own_target) & before, 1, 0), axis=0, keepdims=True
-    )
-    address = own_target * plan.cap_pad + own_slot
-    choose = (address == iota((plan.slots, rows), 0)).astype(jnp.float32).astype(jnp.bfloat16)
     outgoing[...] = (
         jnp.dot(choose, gated, preferred_element_type=jnp.float32)
         .astype(jnp.bfloat16)
@@ -338,12 +345,15 @@
         ),
         in_specs=[
             vmem,
-            pl.BlockSpec(memory_space=pltpu.SMEM),
-            vmem,
+            pl.BlockSpec(memory_space=pltpu.HBM),
+            pl.BlockSpec(memory_space=pltpu.HBM),
             pl.BlockSpec(memory_space=pl.ANY),
         ],
         out_specs=(vmem, vmem),
         scratch_shapes=[
+            pltpu.SMEM(gate_logits.shape, jnp.float32),
+            pltpu.VMEM((rows, width), jnp.bfloat16),
+            pltpu.SemaphoreType.DMA((2,)),
             pltpu.VMEM((n_seq, rows), jnp.int32),
             pltpu.VMEM((plan.chunks, width, CHUNK), jnp.bfloat16),
             pltpu.VMEM((n_seq, plan.cap_pad, width), jnp.bfloat16),
@@ -366,7 +376,7 @@
     )(positions.reshape(1, n_seq * rows), gate_logits, features, proj_weight)
 
     window = plan.window * 8
-    block = 64 if rows_here % 64 == 0 else rows_here
+    block = 128 if rows_here % 128 == 0 else rows_here
     return pl.pallas_call(
         place_kernel,
         grid=(rows_here // block,),

time: 39.9 us -> 39.1 us (0.980)
  Pallas kernels: 37.4 us -> 36.6 us
    pallas_call x1, Pallas kernels: 4.59 us -> 4.03 us  [shards(): pl.pallas_call(place_kernel, grid=(rows_here // block,), out_shape=jax.Sh...]
where the time goes in v4:
time: 39.1 us; the launch traced here: 38.9 us
  Pallas kernels  36.6 us (94%)
  local copies, waits for them, and re-layouts  2.28 us (6%)
    pallas_call x1, Pallas kernels, shards(): pl.pallas_call(functools.partial(join_kernel, plan), out_shape=(jax.Shape...  32.6 us
    pallas_call x1, Pallas kernels, shards(): pl.pallas_call(place_kernel, grid=(rows_here // block,), out_shape=jax.Sh...  4.03 us
    unnamed x6, local copies, waits for them, and re-layouts  1.59 us

profile of v4, /device:TPU:21, one launch (start us, length us, event | category | flops | bytes accessed | tf_op | source)
XLA Modules:
  0.0 38.9 jit_solution(2690610446885911193)
XLA Ops:
  0.0 0.7 %reshape.3.flat_ref = s32[1,576]{1,0:T(1,128)S(1)} reshape(s32[576]{0:T(1024)} %param.8) | data formatting | bytes 4608 | tf_op jit(solution)/shard_map/reshape | solution.py:376
  0.7 0.0 copy-start.1
  0.7 0.9 %copy-done.1 = bf16[72,1344]{1,0:T(8,128)(2,1)S(1)} copy-done((bf16[72,1344]{1,0:T(8,128)(2,1)S(1)}, bf16[72,1344]{1,0:T(8,128)(2,1)}, u32[]{:S(2)}) %copy-start.1) | copy-done | bytes 193560
  1.6 0.0 copy-start.2
  1.6 0.7 %copy-done.2 = f32[1,3]{1,0:T(1,128)S(1)} copy-done((f32[1,3]{1,0:T(1,128)S(1)}, f32[1,3]{1,0:T(1,128)}, u32[]{:S(2)}) %copy-start.2) | copy-done | bytes 36
  2.3 0.0 copy-start
  2.3 32.6 %join.1 = (bf16[3,8,8192]{2,1,0:T(8,128)(2,1)S(1)}, s32[1,24]{1,0:T(1,128)S(1)}) custom-call(s32[1,576]{1,0:T(1,128)S(1)} %reshape.3.flat_ref, f32[1,3]{1,0:T(1,128)S(1)} %copy-done.2, bf16[72,1344]{1,0:T(8,128)(2,1)S(1)} %copy-done.1, bf16[1344,8192]{1,0:T(8,128)(2,1)} %w_ref.1), custom_call_target="tpu_custom_call" | custom-call | tf_op jit(solution)/shard_map/join/pallas_call | solution.py:340
  34.8 0.0 copy-done
  34.9 4.0 %place.1 = bf16[384,8192]{1,0:T(8,128)(2,1)} custom-call(s32[1,24]{1,0:T(1,128)S(1)} %get-tuple-element.7.row_ref, bf16[3,8,8192]{2,1,0:T(8,128)(2,1)S(1)} %get-tuple-element.8.summed_ref, bf16[384,8192]{1,0:T(8,128)(2,1)S(1)} %copy-done), custom_call_target="tpu_custom_call" | custom-call | tf_op jit(solution)/shard_map/place/pallas_call | solution.py:380
Async XLA Ops:
  0.7 0.9 %copy-start.1 = (bf16[72,1344]{1,0:T(8,128)(2,1)S(1)}, bf16[72,1344]{1,0:T(8,128)(2,1)}, u32[]{:S(2)}) copy-start(bf16[72,1344]{1,0:T(8,128)(2,1)} %feat_hbm.1) | copy-start | bytes 580612
  1.6 0.7 %copy-start.2 = (f32[1,3]{1,0:T(1,128)S(1)}, f32[1,3]{1,0:T(1,128)}, u32[]{:S(2)}) copy-start(f32[1,3]{1,0:T(1,128)} %logit_hbm.1) | copy-start | bytes 40
  2.3 32.6 %copy-start = (bf16[384,8192]{1,0:T(8,128)(2,1)S(1)}, bf16[384,8192]{1,0:T(8,128)(2,1)}, u32[]{:S(2)}) copy-start(bf16[384,8192]{1,0:T(8,128)(2,1)} %text_ref.1) | copy-start | bytes 18874372
